TPU v7x, 32 devices: a whole 2x2x4 slice. The times are simulated.
32 devices in a mesh: ctx: 8 (over y, x, core), ch: 4 (over z).
Axes of the slice: x: 2, y: 2, z: 4, core: 2. Of those that a mesh axis runs over, the one named last changes fastest.
Arguments:
- queries: bfloat16 [8192, 2048], P('ch', 'ctx'), may hold values from -6 to 6
- keys: bfloat16 [8192, 2048], P('ch', 'ctx'), may hold values from -6 to 6
- values: bfloat16 [8192, 2048], P('ch', 'ctx'), may hold values from -6 to 6
- short_taps: float32 [3, 7, 8192], P(None, None, 'ch'), may hold values from -2 to 2
- long_filter: bfloat16 [4, 2048, 2048], P('ch', 'ctx'), may hold values from -1.5 to 1.5
- skip_gain: float32 [4, 2048], P('ch', 'ctx'), may hold values from 0.5 to 1.5
Outputs:
- mixed: bfloat16 [8192, 2048], P('ch', 'ctx')
All inputs are finite; a program needn't handle non-finite values.
Results may differ from a plain program's by a relative error of at most 0.01.
Values may be sent and summed in bfloat16 or wider, within the bound.
A program may use at most 64 MiB of HBM per device.

v0:
```python
import math

import jax
import jax.numpy as jnp
from jax import lax
from jax.sharding import PartitionSpec as P

HIGH = lax.Precision.HIGHEST


def passed_along(value, axis, by):
    peers = lax.axis_size(axis)
    pairs = [(i, i + by) for i in range(peers) if 0 <= i + by < peers]
    return lax.ppermute(value, axis, pairs)


def short_conv(extended, taps, length):
    rim = taps.shape[0] - 1
    total = jnp.zeros((extended.shape[0], length), jnp.float32)
    for shift_j in range(taps.shape[0]):
        total = total + taps[shift_j][:, None] * extended[:, rim - shift_j : rim - shift_j + length]
    return total


def split_table(table):
    table_head = table.astype(jnp.bfloat16)
    table_rest = (table - table_head.astype(jnp.float32)).astype(jnp.bfloat16)
    return (table_head, table_rest)


def long_conv(gated, filters, skips):
    channels, length = gated.shape
    size = 2 * length
    cols = 128
    rows = size // cols
    half = rows // 2
    two_pi = 2.0 * math.pi
    row_idx = jnp.arange(rows, dtype=jnp.int32)
    half_idx = jnp.arange(half, dtype=jnp.int32)
    col_idx = jnp.arange(cols, dtype=jnp.int32)
    angle_rows = two_pi * (row_idx[:, None] * half_idx[None, :] % rows).astype(jnp.float32) / rows
    cos_rows, sin_rows = (jnp.cos(angle_rows), jnp.sin(angle_rows))
    cos_head, cos_rest = split_table(cos_rows)
    sin_head, sin_rest = split_table(sin_rows)
    angle_twist = two_pi * (row_idx[:, None] * col_idx[None, :]).astype(jnp.float32) / size
    cos_twist, sin_twist = (jnp.cos(angle_twist), jnp.sin(angle_twist))
    angle_cols = two_pi * (col_idx[:, None] * col_idx[None, :] % cols).astype(jnp.float32) / cols
    cos_cols, sin_cols = (jnp.cos(angle_cols), jnp.sin(angle_cols))

    def first_section(table_head, table_rest, shaped):
        return jnp.einsum(
            "ka,cab->ckb", table_head, shaped, preferred_element_type=jnp.float32
        ) + jnp.einsum("ka,cab->ckb", table_rest, shaped, preferred_element_type=jnp.float32)

    def forward(signal):
        blocks = signal.shape[0]
        shaped = signal.reshape(blocks, half, cols)
        first_re = first_section(cos_head, cos_rest, shaped)
        first_im = -first_section(sin_head, sin_rest, shaped)
        twist_re = first_re * cos_twist + first_im * sin_twist
        twist_im = first_im * cos_twist - first_re * sin_twist
        out_re = jnp.einsum("ckb,bm->ckm", twist_re, cos_cols, precision=HIGH) + jnp.einsum(
            "ckb,bm->ckm", twist_im, sin_cols, precision=HIGH
        )
        out_im = jnp.einsum("ckb,bm->ckm", twist_im, cos_cols, precision=HIGH) - jnp.einsum(
            "ckb,bm->ckm", twist_re, sin_cols, precision=HIGH
        )
        return (out_re, out_im)

    def inverse(spec_re, spec_im):
        blocks = spec_re.shape[0]
        back_re = jnp.einsum("ckm,mb->ckb", spec_re, cos_cols, precision=HIGH) - jnp.einsum(
            "ckm,mb->ckb", spec_im, sin_cols, precision=HIGH
        )
        back_im = jnp.einsum("ckm,mb->ckb", spec_im, cos_cols, precision=HIGH) + jnp.einsum(
            "ckm,mb->ckb", spec_re, sin_cols, precision=HIGH
        )
        turn_re = back_re * cos_twist - back_im * sin_twist
        turn_im = back_re * sin_twist + back_im * cos_twist
        result = jnp.einsum("ka,ckb->cab", cos_rows, turn_re, precision=HIGH) - jnp.einsum(
            "ka,ckb->cab", sin_rows, turn_im, precision=HIGH
        )
        return (result / size).reshape(blocks, length)

    block = math.gcd(channels, 16)
    count = channels // block

    def one_block(triple):
        sig, filt, gain = triple
        sig_re, sig_im = forward(sig)
        filt_re, filt_im = forward(filt)
        prod_re = sig_re * filt_re - sig_im * filt_im
        prod_im = sig_re * filt_im + sig_im * filt_re
        return inverse(prod_re, prod_im) + gain[:, None] * sig.astype(jnp.float32)

    outcome = lax.map(
        one_block,
        (
            gated.reshape(count, block, length),
            filters.reshape(count, block, length),
            skips.reshape(count, block),
        ),
    )
    return outcome.reshape(channels, length).astype(jnp.bfloat16)


def gate_product(first, second):
    return (first.astype(jnp.float32) * second.astype(jnp.float32)).astype(jnp.bfloat16)


def local(queries, keys, values, short_taps, long_filter, skip_gain):
    width, tok_local = queries.shape
    rim = short_taps.shape[1] - 1
    stacked = jnp.stack(
        [queries[:, tok_local - rim :], keys[:, tok_local - rim :], values[:, tok_local - rim :]]
    )
    before = passed_along(stacked, "ctx", 1)

    def extend_home(source, which):
        return jnp.concatenate([before[which], source], axis=1).astype(jnp.float32)

    q_short = short_conv(extend_home(queries, 0), short_taps[0], tok_local).astype(jnp.bfloat16)
    gated = (
        short_conv(extend_home(keys, 1), short_taps[1], tok_local)
        * short_conv(extend_home(values, 2), short_taps[2], tok_local)
    ).astype(jnp.bfloat16)
    g_owned = lax.all_to_all(gated, "ctx", split_axis=0, concat_axis=1, tiled=True)
    outgoing = long_conv(g_owned, long_filter[0], skip_gain[0])
    returned = lax.all_to_all(outgoing, "ctx", split_axis=1, concat_axis=0, tiled=True)
    return gate_product(q_short, returned)


def solution(mesh):
    placed = (
        P("ch", "ctx"),
        P("ch", "ctx"),
        P("ch", "ctx"),
        P(None, None, "ch"),
        P("ch", "ctx", None),
        P("ch", "ctx"),
    )
    return jax.shard_map(
        local, mesh=mesh, in_specs=placed, out_specs=P("ch", "ctx"), check_vma=False
    )
```

profile of v0, /device:TPU:0, one launch (start us, length us, event | category | flops | bytes accessed | tf_op | source)
XLA Modules:
  0.0 269.8 jit_solution(2288781871409935307)
XLA Ops:
  0.0 1.3 slice.190
  1.6 1.3 slice.191
  3.5 2.4 collective-permute-start
  6.1 0.8 collective-permute-done
  7.5 1.3 maximum_convert_fusion.1
  8.8 11.8 %fusion.204 = bf16[2048,256]{1,0:T(8,128)(2,1)} fusion(f32[2048,262]{1,0:T(8,128)S(1)} %get-tuple-element.288, f32[2048,262]{1,0:T(8,128)S(1)} %get-tuple-element.287, f32[2048]{0:T(1024)S(1)} %bitcast.245, f32[2048]{0:T(1024)S(1)} %bitcast.244, f32[2048]{0:T(1024)S(1)} %bitcast.233, f32[2048]{0:T(1024)S(1)} %bitcast.234, f32[2048]{0:T(1024)S(1)} %bitcast.235, ...), kind=kLoop, calls=%fused_computation.203 | loop fusion | flops 14680064 | bytes 30523392 | tf_op jit(solution)/shard_map/convert_element_type | solution.py:126
  20.6 7.9 %all-to-all-start = ((bf16[8,256,256]{2,1,0:T(8,128)(2,1)}), bf16[8,256,256]{2,1,0:T(8,128)(2,1)S(1)}, u32[]{:S(2)}, u32[]{:S(2)}) async-start(bf16[8,256,256]{2,1,0:T(8,128)(2,1)} %bitcast.27), calls=%async_computation | async-start | bytes 2097152 | tf_op jit(solution)/shard_map/all_to_all | solution.py:127
  29.1 0.7 reduce.3
  29.9 14.0 %all-to-all-done = bf16[8,256,256]{2,1,0:T(8,128)(2,1)S(1)} async-done(((bf16[8,256,256]{2,1,0:T(8,128)(2,1)}), bf16[8,256,256]{2,1,0:T(8,128)(2,1)S(1)}, u32[]{:S(2)}, u32[]{:S(2)}) %all-to-all-start) | async-done | bytes 1048608 | tf_op jit(solution)/shard_map/all_to_all | solution.py:127
  45.0 195.2 %while.12 = (s32[]{:T(128)}, bf16[16,16,2048]{2,1,0:T(8,128)(2,1)}, bf16[16,16,2048]{2,1,0:T(8,128)(2,1)S(1)}, bf16[16,16,2048]{2,1,0:T(8,128)(2,1)}, f32[16,16]{1,0:T(8,128)S(1)}, /*index=5*/s32[]{:T(128)}) while((s32[]{:T(128)}, bf16[16,16,2048]{2,1,0:T(8,128)(2,1)}, bf16[16,16,2048]{2,1,0:T(8,128)(2,1)S(1)}, ...), condition=%wide.region_1.2_spmd.clone.clone, body=%wide.region_0.1_spmd.clone.clone.sunk | while | flops 1256058880 | bytes 17597196 | solution.py:96
  45.1 0.9 dynamic-slice_bitcast_fusion.3
  52.6 0.6 multiply_subtract_fusion.16
  56.5 0.7 add_dynamic-update-slice_fusion.2
  57.2 0.8 dynamic-slice_bitcast_fusion.3
  64.8 0.7 multiply_subtract_fusion.16
  68.7 0.7 add_dynamic-update-slice_fusion.2
  69.5 0.8 dynamic-slice_bitcast_fusion.3
  77.0 0.6 multiply_subtract_fusion.16
  80.9 0.7 add_dynamic-update-slice_fusion.2
  81.6 0.8 dynamic-slice_bitcast_fusion.3
  89.2 0.7 multiply_subtract_fusion.16
  93.1 0.7 add_dynamic-update-slice_fusion.2
  93.8 0.8 dynamic-slice_bitcast_fusion.3
  101.4 0.6 multiply_subtract_fusion.16
  105.3 0.7 add_dynamic-update-slice_fusion.2
  106.0 0.8 dynamic-slice_bitcast_fusion.3
  113.6 0.7 multiply_subtract_fusion.16
  117.5 0.7 add_dynamic-update-slice_fusion.2
  118.2 0.8 dynamic-slice_bitcast_fusion.3
  125.8 0.6 multiply_subtract_fusion.16
  129.7 0.7 add_dynamic-update-slice_fusion.2
  130.4 0.8 dynamic-slice_bitcast_fusion.3
  138.0 0.7 multiply_subtract_fusion.16
  141.9 0.7 add_dynamic-update-slice_fusion.2
  142.6 0.8 dynamic-slice_bitcast_fusion.3
  150.2 0.6 multiply_subtract_fusion.16
  154.1 0.7 add_dynamic-update-slice_fusion.2
  154.8 0.8 dynamic-slice_bitcast_fusion.3
  162.4 0.7 multiply_subtract_fusion.16
  166.3 0.7 add_dynamic-update-slice_fusion.2
  167.0 0.8 dynamic-slice_bitcast_fusion.3
  174.6 0.6 multiply_subtract_fusion.16
  178.5 0.7 add_dynamic-update-slice_fusion.2
  179.2 0.8 dynamic-slice_bitcast_fusion.3
  186.8 0.7 multiply_subtract_fusion.16
  190.7 0.7 add_dynamic-update-slice_fusion.2
  191.4 0.8 dynamic-slice_bitcast_fusion.3
  202.9 0.7 add_dynamic-update-slice_fusion.2
  203.6 0.8 dynamic-slice_bitcast_fusion.3
  211.2 0.7 multiply_subtract_fusion.16
  215.1 0.7 add_dynamic-update-slice_fusion.2
  215.8 0.8 dynamic-slice_bitcast_fusion.3
  223.4 0.6 multiply_subtract_fusion.16
  227.3 0.7 add_dynamic-update-slice_fusion.2
  228.0 0.8 dynamic-slice_bitcast_fusion.3
  235.6 0.7 multiply_subtract_fusion.16
  239.5 0.7 add_dynamic-update-slice_fusion.2
  240.2 1.5 copy.29
  241.8 1.2 copy.23
  242.9 4.2 %all-to-all-start.1 = ((bf16[256,8,256]{2,0,1:T(8,128)(2,1)}), bf16[256,8,256]{2,0,1:T(8,128)(2,1)}, u32[]{:S(2)}, u32[]{:S(2)}) async-start(bf16[256,8,256]{2,0,1:T(8,128)(2,1)} %copy.23), calls=%async_computation.1 | async-start | bytes 2097152 | tf_op jit(solution)/shard_map/all_to_all | solution.py:129
  247.2 1.1 copy.19
  248.3 2.0 maximum_convert_fusion
  250.3 12.3 %all-to-all-done.1 = bf16[256,8,256]{2,0,1:T(8,128)(2,1)} async-done(((bf16[256,8,256]{2,0,1:T(8,128)(2,1)}), bf16[256,8,256]{2,0,1:T(8,128)(2,1)}, u32[]{:S(2)}, u32[]{:S(2)}) %all-to-all-start.1) | async-done | bytes 1048608 | tf_op jit(solution)/shard_map/all_to_all | solution.py:129
  262.6 7.2 %fusion.223 = bf16[2048,256]{1,0:T(8,128)(2,1)} fusion(f32[2048,262]{1,0:T(8,128)S(1)} %maximum_convert_fusion, f32[2048]{0:T(1024)S(1)} %bitcast.225, f32[2048]{0:T(1024)S(1)} %bitcast.226, f32[2048]{0:T(1024)S(1)} %bitcast.227, f32[2048]{0:T(1024)S(1)} %bitcast.228, f32[2048]{0:T(1024)S(1)} %bitcast.229, f32[2048]{0:T(1024)S(1)} %bitcast.230, ...), kind=kLoop, calls=%fused_computation.243 | loop fusion | flops 9437184 | bytes 16834560 | tf_op jit(solution)/shard_map/convert_element_type | solution.py:108
  (440 shorter events, 160.5 us)
Async XLA Ops:
  0.0 3.1 %copy-start = (bf16[2048,256]{1,0:T(8,128)(2,1)S(1)}, bf16[2048,256]{1,0:T(8,128)(2,1)}, u32[]{:S(2)}) copy-start(bf16[2048,256]{1,0:T(8,128)(2,1)} %param.10) | copy-start | bytes 3145732
  1.3 4.6 %copy-start.2 = (f32[3,7,2048]{2,1,0:T(8,128)S(1)}, f32[3,7,2048]{2,1,0:T(8,128)}, u32[]{:S(2)}) copy-start(f32[3,7,2048]{2,1,0:T(8,128)} %param.11) | copy-start | bytes 516100
  2.8 4.7 %copy-start.1 = (bf16[2048,256]{1,0:T(8,128)(2,1)S(1)}, bf16[2048,256]{1,0:T(8,128)(2,1)}, u32[]{:S(2)}) copy-start(bf16[2048,256]{1,0:T(8,128)(2,1)} %param.9) | copy-start | bytes 3145732
  3.5 3.3 %collective-permute-start = (bf16[3,2048,6]{1,2,0:T(8,128)(2,1)S(1)}, bf16[3,2048,6]{1,2,0:T(8,128)(2,1)S(1)}, u32[]{:S(2)}, u32[]{:S(2)}) collective-permute-start(bf16[3,2048,6]{1,2,0:T(8,128)(2,1)S(1)} %pad_maximum_fusion), channel_id=1, source_target_pairs={{0,4},{4,8},{8,12},{12,16},{16,20},{20,24},{24,28},{1,5},{5,9},{9,... | collective-permute-start | bytes 221192 | tf_op jit(solution)/shard_map/ppermute | solution.py:14
  20.6 8.5 %copy-start.3 = (f32[1,256]{1,0:T(1,128)S(1)}, f32[1,256]{1,0:T(1,128)}, u32[]{:S(2)}) copy-start(f32[1,256]{1,0:T(1,128)} %param.13) | copy-start | bytes 3076
  20.6 23.3 %all-to-all-start = ((bf16[8,256,256]{2,1,0:T(8,128)(2,1)}), bf16[8,256,256]{2,1,0:T(8,128)(2,1)S(1)}, u32[]{:S(2)}, u32[]{:S(2)}) async-start(bf16[8,256,256]{2,1,0:T(8,128)(2,1)} %bitcast.27), calls=%async_computation | async-start | bytes 2097152 | tf_op jit(solution)/shard_map/all_to_all | solution.py:127
  242.9 19.6 %all-to-all-start.1 = ((bf16[256,8,256]{2,0,1:T(8,128)(2,1)}), bf16[256,8,256]{2,0,1:T(8,128)(2,1)}, u32[]{:S(2)}, u32[]{:S(2)}) async-start(bf16[256,8,256]{2,0,1:T(8,128)(2,1)} %copy.23), calls=%async_computation.1 | async-start | bytes 2097152 | tf_op jit(solution)/shard_map/all_to_all | solution.py:129
where the time goes:
time: 271 us; the launch traced here: 270 us
  matrix products  164 us (61%)
  other arithmetic  35.8 us (13%)
  waiting for transfers between devices  27 us (10%)
  local copies, waits for them, and re-layouts  24.4 us (9%)
  starting transfers between devices  14.6 us (5%)
  loops' own time  3.38 us (1%)
    dot_general x32, matrix products, forward(): jnp.einsum('ckb,bm->ckm', twist_re, sin_cols, precision=HIGH)  20.2 us
    dot_general x32, matrix products, forward(): jnp.einsum('ckb,bm->ckm', twist_im, sin_cols, precision=HIGH)  19.7 us
    dot_general x32, matrix products, forward(): jnp.einsum('ckb,bm->ckm', twist_im, cos_cols, precision=HIGH)  19.5 us
    dot_general x32, matrix products, forward(): jnp.einsum('ckb,bm->ckm', twist_re, cos_cols, precision=HIGH)  19.5 us
    dot_general x64, matrix products, first_section(): jnp.einsum('ka,cab->ckb', table_rest, shaped, preferred_element_type=jnp....  17.9 us
    dot_general x64, matrix products, first_section(): jnp.einsum('ka,cab->ckb', table_head, shaped, preferred_element_type=jnp....  17.5 us
    all_to_all x1, waiting for transfers between devices, local(): lax.all_to_all(gated, 'ctx', split_axis=0, concat_axis=1, tiled=True)  14 us
    while x48, local copies, waits for them, and re-layouts  14 us
  transfers between devices with their start and end apart: 3, of which 3 were waited for; matrix products, arithmetic and copies ran while one was open for 2% of the time, Pallas kernels for 0%

commit v1 on v0

v1 whole, which is shorter than its diff:
```python
import functools
import math

import jax
import jax.numpy as jnp
import ml_dtypes
import numpy as np
from jax import lax
from jax.experimental import pallas as pl
from jax.experimental.pallas import tpu as pltpu
from jax.sharding import PartitionSpec as P

MESH = pl.DeviceIdType.MESH
LANES = 128
SLOT = 8
F32 = jnp.float32
BF16 = jnp.bfloat16


def leaf_angles(count, theta):
    if count == 1:
        return [theta]
    return leaf_angles(count // 2, theta / 2) + leaf_angles(count // 2, theta / 2 + math.pi)


def root_tables(count):
    place = np.arange(LANES, dtype=np.float64)
    tables = []
    for phi in leaf_angles(count, math.pi / 2):
        angle = place[:, None] * (phi + 2.0 * math.pi * place[None, :]) / LANES
        cos, sin = np.cos(angle), np.sin(angle)
        tables.append(np.block([[cos, sin], [-sin, cos]]))
    return np.stack(tables).astype(ml_dtypes.bfloat16)


def split_forward(coefs, theta, first, emit):
    count = len(coefs)
    if count == 1:
        emit(first, *coefs[0])
        return
    half = count // 2
    cos, sin = math.cos(theta / 2), math.sin(theta / 2)
    plus, minus = [], []
    for (lo_re, lo_im), (hi_re, hi_im) in zip(coefs[:half], coefs[half:]):
        if hi_im is None:
            re, im = cos * hi_re, sin * hi_re
            plus.append((lo_re + re, im))
            minus.append((lo_re - re, -im))
        else:
            re, im = cos * hi_re - sin * hi_im, cos * hi_im + sin * hi_re
            plus.append((lo_re + re, lo_im + im))
            minus.append((lo_re - re, lo_im - im))
    split_forward(plus, theta / 2, first, emit)
    split_forward(minus, theta / 2 + math.pi, first + half, emit)


def split_inverse(fetch, count, theta, first, real_only):
    if count == 1:
        return [fetch(first)]
    half = count // 2
    cos, sin = math.cos(theta / 2), math.sin(theta / 2)
    plus = split_inverse(fetch, half, theta / 2, first, False)
    minus = split_inverse(fetch, half, theta / 2 + math.pi, first + half, False)
    low, high = [], []
    for (p_re, p_im), (m_re, m_im) in zip(plus, minus):
        d_re, d_im = p_re - m_re, p_im - m_im
        if real_only:
            low.append((p_re + m_re, None))
            high.append((cos * d_re + sin * d_im, None))
        else:
            low.append((p_re + m_re, p_im + m_im))
            high.append((cos * d_re + sin * d_im, cos * d_im - sin * d_re))
    return low + high


def slot_matrix(shape, lane_axis, off):
    lane = lax.broadcasted_iota(jnp.int32, shape, lane_axis)
    tok = lax.broadcasted_iota(jnp.int32, shape, 1 - lane_axis)
    hit = (lane - tok == off - (LANES - SLOT)) & (tok >= LANES - SLOT)
    return hit.astype(F32).astype(BF16)


def kernel(
    n, chunks,
    q_ref, k_ref, v_ref, taps_ref, filt_ref, gain_ref, table_ref,
    out_ref,
    packed, arrived, halo, taps_t, gated, recv, spec, h_spec, back, outb, ret, qs,
    halo_sem, in_send, in_recv, in_own, out_send, out_recv, out_own,
):
    me = lax.axis_index("ctx")
    width, tok = q_ref.shape
    chan, length = filt_ref.shape
    rows = chan // chunks
    rim = taps_ref.shape[1]
    blocks = length // LANES
    tiles = tok // LANES
    sources = (q_ref, k_ref, v_ref)
    step = 16

    barrier = pltpu.get_barrier_semaphore()
    for d in range(1, n):
        pl.semaphore_signal(barrier, inc=1, device_id={"ctx": lax.rem(me + d, n)}, device_id_type=MESH)

    group = packed.shape[0]
    groups = width // group
    total = jnp.zeros(packed.shape, F32)
    for g in range(groups):
        for w in range(3):
            pick = slot_matrix((LANES, packed.shape[1]), 1, g * 32 + w * SLOT)
            tail = sources[w][g * group : (g + 1) * group, tok - LANES :]
            total = total + jnp.dot(tail, pick, preferred_element_type=F32)
    packed[...] = total.astype(BF16)

    pl.semaphore_wait(barrier, n - 1)

    def taps_step(g, _):
        at = pl.ds(pl.multiple_of(g * LANES, LANES), LANES)
        stack = [taps_ref[w, :, at] for w in range(3)]
        blank = jnp.zeros((SLOT - rim, LANES), F32)
        parts = []
        for one in stack:
            parts += [one, blank]
        parts.append(jnp.zeros((LANES - 3 * SLOT, LANES), F32))
        taps_t[at, :] = jnp.transpose(jnp.concatenate(parts, axis=0))
        return 0

    halo_copy = pltpu.make_async_remote_copy(
        src_ref=packed, dst_ref=arrived, send_sem=halo_sem.at[0], recv_sem=halo_sem.at[1],
        device_id={"ctx": lax.rem(me + 1, n)}, device_id_type=MESH,
    )
    lax.fori_loop(0, width // LANES, taps_step, 0)
    halo_copy.start()

    def emit_at(at):
        def emit(leaf, re, im):
            spec[leaf, at, :LANES] = re.astype(BF16)
            spec[leaf, at, LANES:] = im.astype(BF16)

        return emit

    def filt_step(r, _):
        at = pl.ds(pl.multiple_of(r * step, step), step)
        coefs = [(filt_ref[at, a * LANES : (a + 1) * LANES].astype(F32), None) for a in range(blocks)]
        split_forward(coefs, math.pi / 2, 0, emit_at(at))
        return 0

    lax.fori_loop(0, chan // step, filt_step, 0)

    def filt_leaf(leaf, _):
        h_spec[leaf] = jnp.dot(spec[leaf], table_ref[leaf], preferred_element_type=F32)
        return 0

    lax.fori_loop(0, blocks, filt_leaf, 0)

    halo_copy.wait()
    for g in range(groups):
        for w in range(3):
            spread = slot_matrix((packed.shape[1], LANES), 0, g * 32 + w * SLOT)
            got = jnp.dot(arrived[...], spread, preferred_element_type=F32)
            halo[w, g * group : (g + 1) * group, :] = jnp.where(me > 0, got, 0.0).astype(BF16)

    def short(w, at):
        src = sources[w]
        lane = lax.broadcasted_iota(jnp.int32, (step, LANES), 1)
        parts = [halo[w, at, :].astype(F32)]
        parts += [src[at, t * LANES : (t + 1) * LANES].astype(F32) for t in range(tiles)]
        sums = [None] * tiles
        for j in range(rim):
            tap = jnp.broadcast_to(taps_t[at, w * SLOT + j : w * SLOT + j + 1], (step, LANES))
            turned = parts if j == 0 else [pltpu.roll(p, j, 1) for p in parts]
            for t in range(tiles):
                x = turned[t + 1] if j == 0 else jnp.where(lane < j, turned[t], turned[t + 1])
                sums[t] = tap * x if j == 0 else sums[t] + tap * x
        return sums

    def cols(t):
        return slice(t * LANES, (t + 1) * LANES)

    def gate_rows(base, count):
        def one(r, _):
            at = pl.ds(pl.multiple_of(base + r * step, step), step)
            keys, values = short(1, at), short(2, at)
            for t in range(tiles):
                gated[at, cols(t)] = (keys[t] * values[t]).astype(BF16)
            return 0

        lax.fori_loop(0, count // step, one, 0)

    def peer_rows(peer, c):
        return pl.ds(pl.multiple_of(peer * chan + c * rows, rows), rows)

    def chunk_rows(c):
        return pl.ds(pl.multiple_of(c * rows, rows), rows)

    def in_copy(c, d):
        peer = lax.rem(me + d, n)
        return pltpu.make_async_remote_copy(
            src_ref=gated.at[peer_rows(peer, c), :], dst_ref=recv.at[me, chunk_rows(c), :],
            send_sem=in_send.at[c, d], recv_sem=in_recv.at[c, d],
            device_id={"ctx": peer}, device_id_type=MESH,
        )

    def own_in(c):
        return pltpu.make_async_copy(gated.at[peer_rows(me, c), :], recv.at[me, chunk_rows(c), :], in_own.at[c])

    def out_copy(c, d):
        peer = lax.rem(me + d, n)
        return pltpu.make_async_remote_copy(
            src_ref=outb.at[peer, chunk_rows(c), :], dst_ref=ret.at[peer_rows(me, c), :],
            send_sem=out_send.at[c, d], recv_sem=out_recv.at[c, d],
            device_id={"ctx": peer}, device_id_type=MESH,
        )

    def own_out(c):
        return pltpu.make_async_copy(outb.at[me, chunk_rows(c), :], ret.at[peer_rows(me, c), :], out_own.at[c])

    for c in range(chunks):
        def send_step(d, _):
            gate_rows(lax.rem(me + d, n) * chan + c * rows, rows)

            @pl.when(d > 1)
            def _():
                in_copy(c, d - 1).start()

            return 0

        lax.fori_loop(1, n, send_step, 0)
        gate_rows(me * chan + c * rows, rows)
        in_copy(c, n - 1).start()
        own_in(c).start()

    def q_step(r, _):
        at = pl.ds(pl.multiple_of(r * step, step), step)
        sums = short(0, at)
        for t in range(tiles):
            qs[at, cols(t)] = sums[t].astype(BF16)
        return 0

    lax.fori_loop(0, width // step, q_step, 0)

    for c in range(chunks):
        def wait_in(d, _):
            in_copy(c, d).wait()
            return 0

        lax.fori_loop(1, n, wait_in, 0)
        own_in(c).wait()

        def sig_step(r, _):
            at = pl.ds(pl.multiple_of(c * rows + r * step, step), step)
            coefs = [(recv[a // tiles, at, cols(a % tiles)].astype(F32), None) for a in range(blocks)]
            split_forward(coefs, math.pi / 2, 0, emit_at(at))
            return 0

        lax.fori_loop(0, rows // step, sig_step, 0)

        def leaf_step(leaf, _):
            at = slice(c * rows, (c + 1) * rows)
            table = table_ref[leaf]
            sig = jnp.dot(spec[leaf, at, :], table, preferred_element_type=F32)
            h_re, h_im = h_spec[leaf, at, :LANES], h_spec[leaf, at, LANES:]
            s_re, s_im = sig[:, :LANES], sig[:, LANES:]
            prod = jnp.concatenate([s_re * h_re - s_im * h_im, s_re * h_im + s_im * h_re], axis=1).astype(BF16)
            back[leaf] = lax.dot_general(prod, table, (((1,), (1,)), ((), ())), preferred_element_type=F32)
            return 0

        lax.fori_loop(0, blocks, leaf_step, 0)

        def back_step(r, _):
            at = pl.ds(pl.multiple_of(r * step, step), step)
            whole = pl.ds(pl.multiple_of(c * rows + r * step, step), step)
            row = lax.broadcasted_iota(jnp.int32, (step, chan), 0) + (c * rows + r * step)
            col = lax.broadcasted_iota(jnp.int32, (step, chan), 1)
            gain = jnp.sum(jnp.where(row == col, gain_ref[...], 0.0), axis=1, keepdims=True)
            gain = jnp.broadcast_to(gain, (step, LANES))
            parts = split_inverse(
                lambda leaf: (back[leaf, at, :LANES], back[leaf, at, LANES:]), blocks, math.pi / 2, 0, True
            )
            for a, (re, _unused) in enumerate(parts):
                sig = recv[a // tiles, whole, cols(a % tiles)].astype(F32)
                outb[a // tiles, whole, cols(a % tiles)] = (re * (1.0 / length) + gain * sig).astype(BF16)
            return 0

        lax.fori_loop(0, rows // step, back_step, 0)

        def return_step(d, _):
            out_copy(c, d).start()
            return 0

        lax.fori_loop(1, n, return_step, 0)
        own_out(c).start()

    def mix_rows(base):
        at = pl.ds(pl.multiple_of(base, rows), rows)
        out_ref[at, :] = (qs[at, :].astype(F32) * ret[at, :].astype(F32)).astype(BF16)

    for c in range(chunks):
        own_out(c).wait()
        mix_rows(me * chan + c * rows)

        def mix_step(d, _):
            out_copy(c, d).wait()
            mix_rows(lax.rem(me + n - d, n) * chan + c * rows)
            return 0

        lax.fori_loop(1, n, mix_step, 0)


def solution(mesh):
    n = mesh.shape["ctx"]

    def local(queries, keys, values, short_taps, long_filter, skip_gain):
        width, tok = queries.shape
        chan, length = long_filter.shape[1:]
        blocks = length // LANES
        chunks = 2
        table = jnp.asarray(root_tables(blocks))
        dma = pltpu.SemaphoreType.DMA
        two = 2 * LANES
        groups = 8
        return pl.pallas_call(
            functools.partial(kernel, n, chunks),
            out_shape=jax.ShapeDtypeStruct((width, tok), BF16),
            in_specs=[pl.BlockSpec(memory_space=pltpu.VMEM)] * 7,
            out_specs=pl.BlockSpec(memory_space=pltpu.VMEM),
            scratch_shapes=[
                pltpu.VMEM((width // groups, 32 * groups), BF16),
                pltpu.VMEM((width // groups, 32 * groups), BF16),
                pltpu.VMEM((3, width, LANES), BF16),
                pltpu.VMEM((width, LANES), F32),
                pltpu.VMEM((width, tok), BF16),
                pltpu.VMEM((n, chan, tok), BF16),
                pltpu.VMEM((blocks, chan, two), BF16),
                pltpu.VMEM((blocks, chan, two), F32),
                pltpu.VMEM((blocks, chan // chunks, two), F32),
                pltpu.VMEM((n, chan, tok), BF16),
                pltpu.VMEM((width, tok), BF16),
                pltpu.VMEM((width, tok), BF16),
                dma((2,)),
                dma((chunks, n)),
                dma((chunks, n)),
                dma((chunks,)),
                dma((chunks, n)),
                dma((chunks, n)),
                dma((chunks,)),
            ],
            compiler_params=pltpu.CompilerParams(
                collective_id=0, has_side_effects=True, vmem_limit_bytes=60 * 1024 * 1024
            ),
            name="hyena",
        )(queries, keys, values, short_taps, long_filter[0], skip_gain, table)

    placed = (
        P("ch", "ctx"),
        P("ch", "ctx"),
        P("ch", "ctx"),
        P(None, None, "ch"),
        P("ch", "ctx", None),
        P("ch", "ctx"),
    )
    return jax.shard_map(local, mesh=mesh, in_specs=placed, out_specs=P("ch", "ctx"), check_vma=False)
```

time: 271 us -> 73.4 us (0.27)
  matrix products: 164 us -> 0 us
  Pallas kernels: 0 us -> 70.8 us
  other arithmetic: 35.8 us -> 0 us
  waiting for transfers between devices: 27 us -> 0 us
  local copies, waits for them, and re-layouts: 24.4 us -> 2.26 us
  starting transfers between devices: 14.6 us -> 0 us
  loops' own time: 3.38 us -> 0 us
    dot_general x352 -> x0, matrix products: 164 us -> none  [the longest x32 20.2 us: forward(): jnp.einsum('ckb,bm->ckm', twist_re, sin_cols, precision=HIGH)]
    pallas_call x0 -> x1, Pallas kernels: none -> 70.8 us  [local(): pl.pallas_call(functools.partial(kernel, n, chunks), out_shape=jax.ShapeD...]
    all_to_all x2 -> x0, waiting for transfers between devices: 26.3 us -> none  [the longest x1 14 us: local(): lax.all_to_all(gated, 'ctx', split_axis=0, concat_axis=1, tiled=True)]
    convert_element_type x4 -> x0, other arithmetic: 22.3 us -> none  [the longest x1 11.8 us: local(): gated = (short_conv(extend_home(keys, 1), short_taps[1], tok_local) * sho...]
    while x48 -> x0, local copies, waits for them, and re-layouts: 14 us -> none
    all_to_all x2 -> x0, starting transfers between devices: 12.2 us -> none  [the longest x1 7.94 us: local(): lax.all_to_all(gated, 'ctx', split_axis=0, concat_axis=1, tiled=True)]
    dynamic_update_slice x16 -> x0, other arithmetic: 11.5 us -> none  [long_conv(): lax.map(one_block, (gated.reshape(count, block, length), filters.reshape(...]
    another operation x1 -> x0, loops' own time: 3.38 us -> none  [long_conv(): lax.map(one_block, (gated.reshape(count, block, length), filters.reshape(...]
  transfers between devices with their start and end apart: 3 -> 0, of which waited for: 3 -> 0; matrix products, arithmetic and copies ran while one was open for 2% -> 0% of each run, Pallas kernels for 0% -> 0%
where the time goes in v1:
time: 73.4 us; the launch traced here: 73.1 us
  Pallas kernels  70.8 us (96%)
  local copies, waits for them, and re-layouts  2.26 us (3%)
    pallas_call x1, Pallas kernels, local(): pl.pallas_call(functools.partial(kernel, n, chunks), out_shape=jax.ShapeD...  70.8 us
    unnamed x1, local copies, waits for them, and re-layouts  2.26 us

profile of v1, /device:TPU:0, one launch (start us, length us, event | category | flops | bytes accessed | tf_op | source)
XLA Modules:
  0.0 73.1 jit_solution(6011730269120982644)
XLA Ops:
  0.0 70.8 %hyena.1 = bf16[2048,256]{1,0:T(8,128)(2,1)} custom-call(bf16[2048,256]{1,0:T(8,128)(2,1)} %q_ref.1, bf16[2048,256]{1,0:T(8,128)(2,1)} %k_ref.1, bf16[2048,256]{1,0:T(8,128)(2,1)} %v_ref.1, f32[3,7,2048]{2,1,0:T(8,128)} %taps_ref.1, bf16[256,2048]{1,0:T(8,128)(2,1)} %bitcast.1, f32[1,256]{1,0:T(1,128)} %gain_ref.1, bf16[16,256,256]{2,1,0:T(8,128)(2,1)} %constant.2.clone.table_ref), custom_call_target="tpu_custom_call" | custom-call | tf_op jit(solution)/shard_map/hyena/pallas_call | solution.py:321
  70.9 2.3 %copy.9 = bf16[2048,256]{1,0:T(8,128)(2,1)} copy(bf16[2048,256]{1,0:T(8,128)(2,1)} %hyena.1) | data formatting | bytes 2097152

commit v2 on v1

v2 whole, which is shorter than its diff:
```python
import functools
import math

import jax
import jax.numpy as jnp
import ml_dtypes
import numpy as np
from jax import lax
from jax.experimental import pallas as pl
from jax.experimental.pallas import tpu as pltpu
from jax.sharding import PartitionSpec as P

MESH = pl.DeviceIdType.MESH
LANES = 128
SLOT = 8
F32 = jnp.float32
BF16 = jnp.bfloat16


def leaf_angles(count, theta):
    if count == 1:
        return [theta]
    return leaf_angles(count // 2, theta / 2) + leaf_angles(count // 2, theta / 2 + math.pi)


def root_tables(count):
    place = np.arange(LANES, dtype=np.float64)
    tables = []
    for phi in leaf_angles(count, math.pi / 2):
        angle = place[:, None] * (phi + 2.0 * math.pi * place[None, :]) / LANES
        cos, sin = np.cos(angle), np.sin(angle)
        tables.append(np.block([[cos, sin], [-sin, cos]]).T)
    return np.stack(tables).astype(ml_dtypes.bfloat16)


def split_forward(coefs, theta, first, emit):
    count = len(coefs)
    if count == 1:
        emit(first, *coefs[0])
        return
    half = count // 2
    cos, sin = math.cos(theta / 2), math.sin(theta / 2)
    plus, minus = [], []
    for (lo_re, lo_im), (hi_re, hi_im) in zip(coefs[:half], coefs[half:]):
        if hi_im is None:
            re, im = cos * hi_re, sin * hi_re
            plus.append((lo_re + re, im))
            minus.append((lo_re - re, -im))
        else:
            re, im = cos * hi_re - sin * hi_im, cos * hi_im + sin * hi_re
            plus.append((lo_re + re, lo_im + im))
            minus.append((lo_re - re, lo_im - im))
    split_forward(plus, theta / 2, first, emit)
    split_forward(minus, theta / 2 + math.pi, first + half, emit)


def split_inverse(fetch, count, theta, first, real_only):
    if count == 1:
        return [fetch(first)]
    half = count // 2
    cos, sin = math.cos(theta / 2), math.sin(theta / 2)
    plus = split_inverse(fetch, half, theta / 2, first, False)
    minus = split_inverse(fetch, half, theta / 2 + math.pi, first + half, False)
    low, high = [], []
    for (p_re, p_im), (m_re, m_im) in zip(plus, minus):
        d_re, d_im = p_re - m_re, p_im - m_im
        if real_only:
            low.append((p_re + m_re, None))
            high.append((cos * d_re + sin * d_im, None))
        else:
            low.append((p_re + m_re, p_im + m_im))
            high.append((cos * d_re + sin * d_im, cos * d_im - sin * d_re))
    return low + high


def across(eye, block):
    return lax.dot_general(eye, block, (((1,), (1,)), ((), ())), preferred_element_type=F32)


def kernel(
    n, lanes,
    q_ref, k_ref, v_ref, taps_ref, filt_ref, gain_ref, table_ref,
    out_ref,
    eye, tails, halo, turned, gated, recv, spec, h_spec, ret, back_table,
    halo_sem, in_send, in_recv, in_own, out_send, out_recv, out_own,
):
    me = lax.axis_index("ctx")
    width, tok = q_ref.shape
    chan, length = filt_ref.shape
    chunks = chan // lanes
    rim = taps_ref.shape[-2]
    blocks = length // LANES
    tiles = tok // LANES
    sources = (q_ref, k_ref, v_ref)
    step = 16

    barrier = pltpu.get_barrier_semaphore()
    for d in range(1, n):
        pl.semaphore_signal(barrier, inc=1, device_id={"ctx": lax.rem(me + d, n)}, device_id_type=MESH)

    side = eye.shape[0]
    row = lax.broadcasted_iota(jnp.int32, (side, side), 0)
    col = lax.broadcasted_iota(jnp.int32, (side, side), 1)
    eye[...] = (row == col).astype(F32).astype(BF16)

    pick_row = lax.broadcasted_iota(jnp.int32, (SLOT, LANES), 0) + (LANES - SLOT)
    pick = (pick_row == lax.broadcasted_iota(jnp.int32, (SLOT, LANES), 1)).astype(F32).astype(BF16)

    def tail_step(p, _):
        at = pl.ds(pl.multiple_of(p * chan, chan), chan)
        for w in range(3):
            tails[w, p] = across(pick, sources[w][at, tok - LANES :]).astype(BF16)
        return 0

    lax.fori_loop(0, n, tail_step, 0)

    pl.semaphore_wait(barrier, n - 1)
    halo_copy = pltpu.make_async_remote_copy(
        src_ref=tails, dst_ref=halo, send_sem=halo_sem.at[0], recv_sem=halo_sem.at[1],
        device_id={"ctx": lax.rem(me + 1, n)}, device_id_type=MESH,
    )

    for a in range(blocks):
        gated[a // tiles, (a % tiles) * LANES : (a % tiles + 1) * LANES, :] = across(
            eye[:LANES, :LANES], filt_ref[:, a * LANES : (a + 1) * LANES]
        ).astype(BF16)
    halo_copy.start()

    def short_stage(ref, at_lanes):
        def one(r, _):
            def emit(leaf, re, im):
                spec[leaf, pl.ds(pl.multiple_of(r * step, step), step), at_lanes] = re.astype(BF16)
                spec[leaf, pl.ds(pl.multiple_of(LANES + r * step, step), step), at_lanes] = im.astype(BF16)

            coefs = []
            for a in range(blocks):
                at = pl.ds(pl.multiple_of((a % tiles) * LANES + r * step, step), step)
                coefs.append((ref[a // tiles, at, at_lanes].astype(F32), None))
            split_forward(coefs, math.pi / 2, 0, emit)
            return 0

        lax.fori_loop(0, LANES // step, one, 0)

    def chunk_lanes(c):
        return slice(c * lanes, (c + 1) * lanes)

    for c in range(chunks):
        short_stage(gated, chunk_lanes(c))

    def filt_leaf(leaf, _):
        table = table_ref[leaf]
        h_spec[leaf] = jnp.dot(table, spec[leaf], preferred_element_type=F32).astype(h_spec.dtype)
        if back_table.shape[0] == blocks:
            back_table[leaf] = across(eye[: 2 * LANES, : 2 * LANES], table).astype(BF16)
        return 0

    lax.fori_loop(0, blocks, filt_leaf, 0, unroll=2)

    halo_copy.wait()

    def peer_rows(peer, c):
        return pl.ds(pl.multiple_of(peer * chan + c * lanes, lanes), lanes)

    def short(w, peer, c):
        turned[w, :SLOT, :] = jnp.where(me > 0, halo[w, peer, :, chunk_lanes(c)].astype(F32), 0.0)
        turned[w, SLOT:, :] = across(eye[:tok, :tok], sources[w][peer_rows(peer, c), :])
        if len(taps_ref.shape) == 3:
            taps = taps_ref[w, :, peer_rows(peer, c)]
        else:
            taps = taps_ref[peer, w, :, chunk_lanes(c)]
        return taps

    def sums_of(w, taps, start, count):
        total = None
        for j in range(rim):
            term = taps[j : j + 1, :] * turned[w, SLOT - j + start : SLOT - j + start + count, :]
            total = term if total is None else total + term
        return total

    part = 64

    def gate(peer, c):
        k_taps, v_taps = short(1, peer, c), short(2, peer, c)
        for start in range(0, tok, part):
            product = sums_of(1, k_taps, start, part) * sums_of(2, v_taps, start, part)
            gated[peer, start : start + part, chunk_lanes(c)] = product.astype(BF16)

    def in_copy(c, d):
        peer = lax.rem(me + d, n)
        return pltpu.make_async_remote_copy(
            src_ref=gated.at[peer, :, chunk_lanes(c)], dst_ref=recv.at[me, :, chunk_lanes(c)],
            send_sem=in_send.at[c, d], recv_sem=in_recv.at[c, d],
            device_id={"ctx": peer}, device_id_type=MESH,
        )

    def own_in(c):
        return pltpu.make_async_copy(gated.at[me, :, chunk_lanes(c)], recv.at[me, :, chunk_lanes(c)], in_own.at[c])

    def out_copy(c, d):
        peer = lax.rem(me + d, n)
        return pltpu.make_async_remote_copy(
            src_ref=recv.at[peer, :, chunk_lanes(c)], dst_ref=ret.at[me, :, chunk_lanes(c)],
            send_sem=out_send.at[c, d], recv_sem=out_recv.at[c, d],
            device_id={"ctx": peer}, device_id_type=MESH,
        )

    def own_out(c):
        return pltpu.make_async_copy(recv.at[me, :, chunk_lanes(c)], ret.at[me, :, chunk_lanes(c)], out_own.at[c])

    for c in range(chunks):
        def send_step(d, _):
            gate(lax.rem(me + d, n), c)

            @pl.when(d > 1)
            def _():
                in_copy(c, d - 1).start()

            return 0

        lax.fori_loop(1, n, send_step, 0)
        gate(me, c)
        in_copy(c, n - 1).start()
        own_in(c).start()

    for c in range(chunks):
        def q_step(p, _):
            taps = short(0, p, c)
            parts = [sums_of(0, taps, start, part).astype(BF16) for start in range(0, tok, part)]
            out_ref[peer_rows(p, c), :] = across(eye[:lanes, :lanes], jnp.concatenate(parts, axis=0)).astype(BF16)
            return 0

        lax.fori_loop(0, n, q_step, 0)

    for c in range(chunks):
        def wait_in(d, _):
            in_copy(c, d).wait()
            return 0

        lax.fori_loop(1, n, wait_in, 0)
        own_in(c).wait()
        at_lanes = chunk_lanes(c)
        short_stage(recv, at_lanes)

        def leaf_step(leaf, _):
            table = table_ref[leaf]
            if back_table.shape[0] == blocks:
                turn = back_table[leaf]
            else:
                turn = across(eye[: 2 * LANES, : 2 * LANES], table).astype(BF16)
            sig = jnp.dot(table, spec[leaf, :, at_lanes], preferred_element_type=F32)
            h_re, h_im = h_spec[leaf, :LANES, at_lanes].astype(F32), h_spec[leaf, LANES:, at_lanes].astype(F32)
            s_re, s_im = sig[:LANES], sig[LANES:]
            prod = jnp.concatenate([s_re * h_re - s_im * h_im, s_re * h_im + s_im * h_re], axis=0).astype(BF16)
            h_spec[leaf, :, at_lanes] = jnp.dot(turn, prod, preferred_element_type=F32).astype(h_spec.dtype)
            return 0

        lax.fori_loop(0, blocks, leaf_step, 0, unroll=4)
        gain = gain_ref[:, at_lanes]

        def back_step(r, _):
            re_at = pl.ds(pl.multiple_of(r * step, step), step)
            im_at = pl.ds(pl.multiple_of(LANES + r * step, step), step)
            parts = split_inverse(
                lambda leaf: (h_spec[leaf, re_at, at_lanes].astype(F32), h_spec[leaf, im_at, at_lanes].astype(F32)),
                blocks, math.pi / 2, 0, True,
            )
            for a, (re, _unused) in enumerate(parts):
                at = pl.ds(pl.multiple_of((a % tiles) * LANES + r * step, step), step)
                sig = recv[a // tiles, at, at_lanes].astype(F32)
                recv[a // tiles, at, at_lanes] = (re * (1.0 / length) + gain * sig).astype(BF16)
            return 0

        lax.fori_loop(0, LANES // step, back_step, 0)

        def return_step(d, _):
            out_copy(c, d).start()
            return 0

        lax.fori_loop(1, n, return_step, 0)
        own_out(c).start()

    def mix(peer, c):
        at = peer_rows(peer, c)
        long = across(eye[:lanes, :lanes], ret[peer, :, chunk_lanes(c)])
        out_ref[at, :] = (out_ref[at, :].astype(F32) * long).astype(BF16)

    for c in range(chunks):
        own_out(c).wait()
        mix(me, c)

        def mix_step(d, _):
            out_copy(c, d).wait()
            mix(lax.rem(me + n - d, n), c)
            return 0

        lax.fori_loop(1, n, mix_step, 0)


def solution(mesh):
    n = mesh.shape["ctx"]

    def local(queries, keys, values, short_taps, long_filter, skip_gain):
        width, tok = queries.shape
        chan, length = long_filter.shape[1:]
        blocks = length // LANES
        lanes = min(chan, LANES)
        chunks = chan // lanes
        table = jnp.asarray(root_tables(blocks))
        dma = pltpu.SemaphoreType.DMA
        two = 2 * LANES
        small = blocks * two * max(chan, LANES) * 4 <= 8 * 2**20
        side = max(tok, two)
        taps = short_taps
        if lanes < LANES:
            taps = jnp.moveaxis(short_taps.reshape(3, -1, n, chan), 2, 0)
        return pl.pallas_call(
            functools.partial(kernel, n, lanes),
            out_shape=jax.ShapeDtypeStruct((width, tok), BF16),
            in_specs=[pl.BlockSpec(memory_space=pltpu.VMEM)] * 7,
            out_specs=pl.BlockSpec(memory_space=pltpu.VMEM),
            scratch_shapes=[
                pltpu.VMEM((side, side), BF16),
                pltpu.VMEM((3, n, SLOT, chan), BF16),
                pltpu.VMEM((3, n, SLOT, chan), BF16),
                pltpu.VMEM((3, SLOT + tok, lanes), F32),
                pltpu.VMEM((n, tok, chan), BF16),
                pltpu.VMEM((n, tok, chan), BF16),
                pltpu.VMEM((blocks, two, chan), BF16),
                pltpu.VMEM((blocks, two, chan), F32 if small else BF16),
                pltpu.VMEM((n, tok, chan), BF16),
                pltpu.VMEM((blocks if small else 1, two, two), BF16),
                dma((2,)),
                dma((chunks, n)),
                dma((chunks, n)),
                dma((chunks,)),
                dma((chunks, n)),
                dma((chunks, n)),
                dma((chunks,)),
            ],
            compiler_params=pltpu.CompilerParams(
                collective_id=0, has_side_effects=True, vmem_limit_bytes=67043328
            ),
            name="hyena",
        )(queries, keys, values, taps, long_filter[0], skip_gain, table)

    placed = (
        P("ch", "ctx"),
        P("ch", "ctx"),
        P("ch", "ctx"),
        P(None, None, "ch"),
        P("ch", "ctx", None),
        P("ch", "ctx"),
    )
    return jax.shard_map(local, mesh=mesh, in_specs=placed, out_specs=P("ch", "ctx"), check_vma=False)
```

time: 73.4 us -> 44.2 us (0.60)
  Pallas kernels: 70.8 us -> 41.8 us
    pallas_call x1, Pallas kernels: 70.8 us -> 41.8 us  [local(): pl.pallas_call(functools.partial(kernel, n, lanes), out_shape=jax.ShapeDt...]
where the time goes in v2:
time: 44.2 us; the launch traced here: 44.1 us
  Pallas kernels  41.8 us (95%)
  local copies, waits for them, and re-layouts  2.26 us (5%)
    pallas_call x1, Pallas kernels, local(): pl.pallas_call(functools.partial(kernel, n, lanes), out_shape=jax.ShapeDt...  41.8 us
    unnamed x1, local copies, waits for them, and re-layouts  2.26 us

profile of v2, /device:TPU:0, one launch (start us, length us, event | category | flops | bytes accessed | tf_op | source)
XLA Modules:
  0.0 44.1 jit_solution(7515886510925122279)
XLA Ops:
  0.0 41.8 %hyena.1 = bf16[2048,256]{1,0:T(8,128)(2,1)} custom-call(bf16[2048,256]{1,0:T(8,128)(2,1)} %q_ref.1, bf16[2048,256]{1,0:T(8,128)(2,1)} %k_ref.1, bf16[2048,256]{1,0:T(8,128)(2,1)} %v_ref.1, f32[3,7,2048]{2,1,0:T(8,128)} %taps_ref.1, bf16[256,2048]{1,0:T(8,128)(2,1)} %bitcast.1, f32[1,256]{1,0:T(1,128)} %gain_ref.1, bf16[16,256,256]{2,1,0:T(8,128)(2,1)} %constant.2.clone.table_ref), custom_call_target="tpu_custom_call" | custom-call | tf_op jit(solution)/shard_map/hyena/pallas_call | solution.py:316
  41.8 2.3 %copy.9 = bf16[2048,256]{1,0:T(8,128)(2,1)} copy(bf16[2048,256]{1,0:T(8,128)(2,1)} %hyena.1) | data formatting | bytes 2097152

commit v3 on v2

--- a/solution.py
+++ b/solution.py
@@ -23,14 +23,17 @@
     return leaf_angles(count // 2, theta / 2) + leaf_angles(count // 2, theta / 2 + math.pi)
 
 
-def root_tables(count):
+def circle_tables():
     place = np.arange(LANES, dtype=np.float64)
-    tables = []
-    for phi in leaf_angles(count, math.pi / 2):
-        angle = place[:, None] * (phi + 2.0 * math.pi * place[None, :]) / LANES
-        cos, sin = np.cos(angle), np.sin(angle)
-        tables.append(np.block([[cos, sin], [-sin, cos]]).T)
-    return np.stack(tables).astype(ml_dtypes.bfloat16)
+    angle = place[:, None] * place[None, :] * (2.0 * math.pi / LANES)
+    cos, sin = np.cos(angle), np.sin(angle)
+    there = np.block([[cos, -sin], [sin, cos]])
+    return np.stack([there, there.T]).astype(ml_dtypes.bfloat16)
+
+
+def twist_columns(count):
+    angle = np.arange(LANES)[:, None] * np.array(leaf_angles(count, math.pi / 2))[None, :] / LANES
+    return np.concatenate([np.cos(angle), np.sin(angle)], axis=1).astype(np.float32)
 
 
 def split_forward(coefs, theta, first, emit):
@@ -79,10 +82,10 @@
 
 def kernel(
     n, lanes,
-    q_ref, k_ref, v_ref, taps_ref, filt_ref, gain_ref, table_ref,
+    q_ref, k_ref, v_ref, taps_ref, filt_hbm, gain_ref, table_ref, twist_ref,
     out_ref,
-    eye, tails, halo, turned, gated, recv, spec, h_spec, ret, back_table,
-    halo_sem, in_send, in_recv, in_own, out_send, out_recv, out_own,
+    eye, tails, halo, turned, gated, recv, spec, h_spec, ret, filt_ref, filt_rows, twist,
+    filt_sem, halo_sem, in_send, in_recv, in_own, out_send, out_recv, out_own,
 ):
     me = lax.axis_index("ctx")
     width, tok = q_ref.shape
@@ -93,6 +96,8 @@
     tiles = tok // LANES
     sources = (q_ref, k_ref, v_ref)
     step = 16
+    filt_copy = pltpu.make_async_copy(filt_hbm, filt_ref, filt_sem)
+    filt_copy.start()
 
     barrier = pltpu.get_barrier_semaphore()
     for d in range(1, n):
@@ -120,17 +125,37 @@
         device_id={"ctx": lax.rem(me + 1, n)}, device_id_type=MESH,
     )
 
+    for leaf in range(blocks):
+        for part in range(2):
+            column = twist_ref[:, part * blocks + leaf : part * blocks + leaf + 1]
+            twist[leaf, part] = jnp.broadcast_to(column, (LANES, lanes))
+    halo_copy.start()
+    if lanes < LANES:
+        spec[...] = jnp.zeros_like(spec)
+
+    filt_copy.wait()
     for a in range(blocks):
-        gated[a // tiles, (a % tiles) * LANES : (a % tiles + 1) * LANES, :] = across(
+        filt_rows[a // tiles, (a % tiles) * LANES : (a % tiles + 1) * LANES, :] = across(
             eye[:LANES, :LANES], filt_ref[:, a * LANES : (a + 1) * LANES]
         ).astype(BF16)
-    halo_copy.start()
-
-    def short_stage(ref, at_lanes):
+
+    def chunk_lanes(c):
+        return slice(c * lanes, (c + 1) * lanes)
+
+    def leaf_lanes(leaf):
+        return slice((leaf % 2) * LANES, (leaf % 2) * LANES + lanes)
+
+    def short_stage(ref, c):
+        at_lanes = chunk_lanes(c)
+
         def one(r, _):
+            re_at = pl.ds(pl.multiple_of(r * step, step), step)
+            im_at = pl.ds(pl.multiple_of(LANES + r * step, step), step)
+
             def emit(leaf, re, im):
-                spec[leaf, pl.ds(pl.multiple_of(r * step, step), step), at_lanes] = re.astype(BF16)
-                spec[leaf, pl.ds(pl.multiple_of(LANES + r * step, step), step), at_lanes] = im.astype(BF16)
+                cos, sin = twist[leaf, 0, re_at, :], twist[leaf, 1, re_at, :]
+                spec[leaf // 2, re_at, leaf_lanes(leaf)] = (re * cos - im * sin).astype(BF16)
+                spec[leaf // 2, im_at, leaf_lanes(leaf)] = (re * sin + im * cos).astype(BF16)
 
             coefs = []
             for a in range(blocks):
@@ -141,49 +166,43 @@
 
         lax.fori_loop(0, LANES // step, one, 0)
 
-    def chunk_lanes(c):
-        return slice(c * lanes, (c + 1) * lanes)
-
-    for c in range(chunks):
-        short_stage(gated, chunk_lanes(c))
-
-    def filt_leaf(leaf, _):
-        table = table_ref[leaf]
-        h_spec[leaf] = jnp.dot(table, spec[leaf], preferred_element_type=F32).astype(h_spec.dtype)
-        if back_table.shape[0] == blocks:
-            back_table[leaf] = across(eye[: 2 * LANES, : 2 * LANES], table).astype(BF16)
-        return 0
-
-    lax.fori_loop(0, blocks, filt_leaf, 0, unroll=2)
-
+    def filter_chunk(c):
+        short_stage(filt_rows, c)
+
+        def filt_pair(pair, _):
+            h_spec[c, pair] = jnp.dot(table_ref[0], spec[pair], preferred_element_type=F32).astype(h_spec.dtype)
+            return 0
+
+        lax.fori_loop(0, blocks // 2, filt_pair, 0, unroll=2)
+
+    filter_chunk(0)
     halo_copy.wait()
 
     def peer_rows(peer, c):
         return pl.ds(pl.multiple_of(peer * chan + c * lanes, lanes), lanes)
 
-    def short(w, peer, c):
-        turned[w, :SLOT, :] = jnp.where(me > 0, halo[w, peer, :, chunk_lanes(c)].astype(F32), 0.0)
-        turned[w, SLOT:, :] = across(eye[:tok, :tok], sources[w][peer_rows(peer, c), :])
+    def short(w, slot, peer, c):
+        turned[slot, :SLOT, :] = jnp.where(me > 0, halo[w, peer, :, chunk_lanes(c)].astype(F32), 0.0)
+        turned[slot, SLOT:, :] = across(eye[:tok, :tok], sources[w][peer_rows(peer, c), :])
         if len(taps_ref.shape) == 3:
-            taps = taps_ref[w, :, peer_rows(peer, c)]
-        else:
-            taps = taps_ref[peer, w, :, chunk_lanes(c)]
-        return taps
-
-    def sums_of(w, taps, start, count):
+            return taps_ref[w, :, peer_rows(peer, c)]
+        return taps_ref[peer, w, :, chunk_lanes(c)]
+
+    def sums_of(slot, taps, start, count):
         total = None
         for j in range(rim):
-            term = taps[j : j + 1, :] * turned[w, SLOT - j + start : SLOT - j + start + count, :]
+            term = taps[j : j + 1, :] * turned[slot, SLOT - j + start : SLOT - j + start + count, :]
             total = term if total is None else total + term
         return total
 
     part = 64
 
-    def gate(peer, c):
-        k_taps, v_taps = short(1, peer, c), short(2, peer, c)
-        for start in range(0, tok, part):
-            product = sums_of(1, k_taps, start, part) * sums_of(2, v_taps, start, part)
-            gated[peer, start : start + part, chunk_lanes(c)] = product.astype(BF16)
+    def gate_pair(peers, c):
+        taps = [(short(1, 2 * i, p, c), short(2, 2 * i + 1, p, c)) for i, p in enumerate(peers)]
+        for i, p in enumerate(peers):
+            for start in range(0, tok, part):
+                product = sums_of(2 * i, taps[i][0], start, part) * sums_of(2 * i + 1, taps[i][1], start, part)
+                gated[p, start : start + part, chunk_lanes(c)] = product.astype(BF16)
 
     def in_copy(c, d):
         peer = lax.rem(me + d, n)
@@ -208,28 +227,22 @@
         return pltpu.make_async_copy(recv.at[me, :, chunk_lanes(c)], ret.at[me, :, chunk_lanes(c)], out_own.at[c])
 
     for c in range(chunks):
-        def send_step(d, _):
-            gate(lax.rem(me + d, n), c)
-
-            @pl.when(d > 1)
+        def send_step(i, _):
+            gate_pair([lax.rem(me + 2 * i + 1, n), lax.rem(me + 2 * i + 2, n)], c)
+
+            @pl.when(i > 0)
             def _():
-                in_copy(c, d - 1).start()
-
-            return 0
-
-        lax.fori_loop(1, n, send_step, 0)
-        gate(me, c)
+                in_copy(c, 2 * i - 1).start()
+                in_copy(c, 2 * i).start()
+
+            return 0
+
+        lax.fori_loop(0, n // 2, send_step, 0)
         in_copy(c, n - 1).start()
         own_in(c).start()
 
-    for c in range(chunks):
-        def q_step(p, _):
-            taps = short(0, p, c)
-            parts = [sums_of(0, taps, start, part).astype(BF16) for start in range(0, tok, part)]
-            out_ref[peer_rows(p, c), :] = across(eye[:lanes, :lanes], jnp.concatenate(parts, axis=0)).astype(BF16)
-            return 0
-
-        lax.fori_loop(0, n, q_step, 0)
+    for c in range(1, chunks):
+        filter_chunk(c)
 
     for c in range(chunks):
         def wait_in(d, _):
@@ -239,31 +252,29 @@
         lax.fori_loop(1, n, wait_in, 0)
         own_in(c).wait()
         at_lanes = chunk_lanes(c)
-        short_stage(recv, at_lanes)
-
-        def leaf_step(leaf, _):
-            table = table_ref[leaf]
-            if back_table.shape[0] == blocks:
-                turn = back_table[leaf]
-            else:
-                turn = across(eye[: 2 * LANES, : 2 * LANES], table).astype(BF16)
-            sig = jnp.dot(table, spec[leaf, :, at_lanes], preferred_element_type=F32)
-            h_re, h_im = h_spec[leaf, :LANES, at_lanes].astype(F32), h_spec[leaf, LANES:, at_lanes].astype(F32)
+        short_stage(recv, c)
+
+        def pair_step(pair, _):
+            sig = jnp.dot(table_ref[0], spec[pair], preferred_element_type=F32)
+            h_re, h_im = h_spec[c, pair, :LANES, :].astype(F32), h_spec[c, pair, LANES:, :].astype(F32)
             s_re, s_im = sig[:LANES], sig[LANES:]
             prod = jnp.concatenate([s_re * h_re - s_im * h_im, s_re * h_im + s_im * h_re], axis=0).astype(BF16)
-            h_spec[leaf, :, at_lanes] = jnp.dot(turn, prod, preferred_element_type=F32).astype(h_spec.dtype)
-            return 0
-
-        lax.fori_loop(0, blocks, leaf_step, 0, unroll=4)
+            h_spec[c, pair] = jnp.dot(table_ref[1], prod, preferred_element_type=F32).astype(h_spec.dtype)
+            return 0
+
+        lax.fori_loop(0, blocks // 2, pair_step, 0, unroll=4)
         gain = gain_ref[:, at_lanes]
 
         def back_step(r, _):
             re_at = pl.ds(pl.multiple_of(r * step, step), step)
             im_at = pl.ds(pl.multiple_of(LANES + r * step, step), step)
-            parts = split_inverse(
-                lambda leaf: (h_spec[leaf, re_at, at_lanes].astype(F32), h_spec[leaf, im_at, at_lanes].astype(F32)),
-                blocks, math.pi / 2, 0, True,
-            )
+            def fetch(leaf):
+                re = h_spec[c, leaf // 2, re_at, leaf_lanes(leaf)].astype(F32)
+                im = h_spec[c, leaf // 2, im_at, leaf_lanes(leaf)].astype(F32)
+                cos, sin = twist[leaf, 0, re_at, :], twist[leaf, 1, re_at, :]
+                return re * cos + im * sin, im * cos - re * sin
+
+            parts = split_inverse(fetch, blocks, math.pi / 2, 0, True)
             for a, (re, _unused) in enumerate(parts):
                 at = pl.ds(pl.multiple_of((a % tiles) * LANES + r * step, step), step)
                 sig = recv[a // tiles, at, at_lanes].astype(F32)
@@ -278,6 +289,17 @@
 
         lax.fori_loop(1, n, return_step, 0)
         own_out(c).start()
+
+    for c in range(chunks):
+        def q_step(i, _):
+            peers = (2 * i, 2 * i + 1)
+            taps = [short(0, slot, p, c) for slot, p in enumerate(peers)]
+            for slot, p in enumerate(peers):
+                parts = [sums_of(slot, taps[slot], start, part).astype(BF16) for start in range(0, tok, part)]
+                out_ref[peer_rows(p, c), :] = across(eye[:lanes, :lanes], jnp.concatenate(parts, axis=0)).astype(BF16)
+            return 0
+
+        lax.fori_loop(0, n // 2, q_step, 0)
 
     def mix(peer, c):
         at = peer_rows(peer, c)
@@ -305,30 +327,35 @@
         blocks = length // LANES
         lanes = min(chan, LANES)
         chunks = chan // lanes
-        table = jnp.asarray(root_tables(blocks))
+        table = jnp.asarray(circle_tables())
+        columns = jnp.asarray(twist_columns(blocks))
         dma = pltpu.SemaphoreType.DMA
         two = 2 * LANES
         small = blocks * two * max(chan, LANES) * 4 <= 8 * 2**20
-        side = max(tok, two)
+        side = max(tok, LANES)
+        any_space = pl.BlockSpec(memory_space=pl.ANY)
         taps = short_taps
         if lanes < LANES:
             taps = jnp.moveaxis(short_taps.reshape(3, -1, n, chan), 2, 0)
         return pl.pallas_call(
             functools.partial(kernel, n, lanes),
             out_shape=jax.ShapeDtypeStruct((width, tok), BF16),
-            in_specs=[pl.BlockSpec(memory_space=pltpu.VMEM)] * 7,
+            in_specs=[any_space if i == 4 else pl.BlockSpec(memory_space=pltpu.VMEM) for i in range(8)],
             out_specs=pl.BlockSpec(memory_space=pltpu.VMEM),
             scratch_shapes=[
                 pltpu.VMEM((side, side), BF16),
                 pltpu.VMEM((3, n, SLOT, chan), BF16),
                 pltpu.VMEM((3, n, SLOT, chan), BF16),
-                pltpu.VMEM((3, SLOT + tok, lanes), F32),
+                pltpu.VMEM((4, SLOT + tok, lanes), F32),
                 pltpu.VMEM((n, tok, chan), BF16),
                 pltpu.VMEM((n, tok, chan), BF16),
-                pltpu.VMEM((blocks, two, chan), BF16),
-                pltpu.VMEM((blocks, two, chan), F32 if small else BF16),
+                pltpu.VMEM((blocks // 2, two, two), BF16),
+                pltpu.VMEM((chunks, blocks // 2, two, two), F32 if small else BF16),
                 pltpu.VMEM((n, tok, chan), BF16),
-                pltpu.VMEM((blocks if small else 1, two, two), BF16),
+                pltpu.VMEM((chan, length), BF16),
+                pltpu.VMEM((n, tok, chan), BF16),
+                pltpu.VMEM((blocks, 2, LANES, lanes), F32),
+                dma,
                 dma((2,)),
                 dma((chunks, n)),
                 dma((chunks, n)),
@@ -341,7 +368,7 @@
                 collective_id=0, has_side_effects=True, vmem_limit_bytes=67043328
             ),
             name="hyena",
-        )(queries, keys, values, taps, long_filter[0], skip_gain, table)
+        )(queries, keys, values, taps, long_filter[0], skip_gain, table, columns)
 
     placed = (
         P("ch", "ctx"),

time: 44.2 us -> 39.3 us (0.89)
  Pallas kernels: 41.8 us -> 36.8 us
    pallas_call x1, Pallas kernels: 41.8 us -> 36.8 us  [local(): pl.pallas_call(functools.partial(kernel, n, lanes), out_shape=jax.ShapeDt...]
where the time goes in v3:
time: 39.3 us; the launch traced here: 39.1 us
  Pallas kernels  36.8 us (94%)
  local copies, waits for them, and re-layouts  2.26 us (6%)
    pallas_call x1, Pallas kernels, local(): pl.pallas_call(functools.partial(kernel, n, lanes), out_shape=jax.ShapeDt...  36.8 us
    unnamed x1, local copies, waits for them, and re-layouts  2.26 us

profile of v3, /device:TPU:0, one launch (start us, length us, event | category | flops | bytes accessed | tf_op | source)
XLA Modules:
  0.0 39.1 jit_solution(10381110632918520222)
XLA Ops:
  0.0 36.8 %hyena.1 = bf16[2048,256]{1,0:T(8,128)(2,1)} custom-call(bf16[2048,256]{1,0:T(8,128)(2,1)} %q_ref.1, bf16[2048,256]{1,0:T(8,128)(2,1)} %k_ref.1, bf16[2048,256]{1,0:T(8,128)(2,1)} %v_ref.1, f32[3,7,2048]{2,1,0:T(8,128)} %taps_ref.1, bf16[256,2048]{1,0:T(8,128)(2,1)} %bitcast.1, f32[1,256]{1,0:T(1,128)} %gain_ref.1, ...), custom_call_target="tpu_custom_call" | custom-call | tf_op jit(solution)/shard_map/hyena/pallas_call | solution.py:340
  36.8 2.3 %copy.10 = bf16[2048,256]{1,0:T(8,128)(2,1)} copy(bf16[2048,256]{1,0:T(8,128)(2,1)} %hyena.1) | data formatting | bytes 2097152

commit v4 on v3

--- a/solution.py
+++ b/solution.py
@@ -32,8 +32,20 @@
 
 
 def twist_columns(count):
-    angle = np.arange(LANES)[:, None] * np.array(leaf_angles(count, math.pi / 2))[None, :] / LANES
+    roots = np.array(leaf_angles(count, 0.0)) + math.pi / (2 * count)
+    angle = np.arange(LANES)[:, None] * roots[None, :] / LANES
     return np.concatenate([np.cos(angle), np.sin(angle)], axis=1).astype(np.float32)
+
+
+def turn(re, im, angle):
+    eighth = round(angle / (math.pi / 4))
+    if abs(angle - eighth * math.pi / 4) > 1e-9:
+        cos, sin = math.cos(angle), math.sin(angle)
+        return cos * re - sin * im, cos * im + sin * re
+    eighth %= 8
+    if eighth % 2:
+        re, im = math.sqrt(0.5) * (re - im), math.sqrt(0.5) * (re + im)
+    return [(re, im), (-im, re), (-re, -im), (im, -re)][eighth // 2]
 
 
 def split_forward(coefs, theta, first, emit):
@@ -42,37 +54,25 @@
         emit(first, *coefs[0])
         return
     half = count // 2
-    cos, sin = math.cos(theta / 2), math.sin(theta / 2)
     plus, minus = [], []
-    for (lo_re, lo_im), (hi_re, hi_im) in zip(coefs[:half], coefs[half:]):
-        if hi_im is None:
-            re, im = cos * hi_re, sin * hi_re
-            plus.append((lo_re + re, im))
-            minus.append((lo_re - re, -im))
-        else:
-            re, im = cos * hi_re - sin * hi_im, cos * hi_im + sin * hi_re
-            plus.append((lo_re + re, lo_im + im))
-            minus.append((lo_re - re, lo_im - im))
+    for (lo_re, lo_im), high in zip(coefs[:half], coefs[half:]):
+        hi_re, hi_im = turn(*high, theta / 2)
+        plus.append((lo_re + hi_re, lo_im + hi_im))
+        minus.append((lo_re - hi_re, lo_im - hi_im))
     split_forward(plus, theta / 2, first, emit)
     split_forward(minus, theta / 2 + math.pi, first + half, emit)
 
 
-def split_inverse(fetch, count, theta, first, real_only):
+def split_inverse(fetch, count, theta, first):
     if count == 1:
         return [fetch(first)]
     half = count // 2
-    cos, sin = math.cos(theta / 2), math.sin(theta / 2)
-    plus = split_inverse(fetch, half, theta / 2, first, False)
-    minus = split_inverse(fetch, half, theta / 2 + math.pi, first + half, False)
+    plus = split_inverse(fetch, half, theta / 2, first)
+    minus = split_inverse(fetch, half, theta / 2 + math.pi, first + half)
     low, high = [], []
     for (p_re, p_im), (m_re, m_im) in zip(plus, minus):
-        d_re, d_im = p_re - m_re, p_im - m_im
-        if real_only:
-            low.append((p_re + m_re, None))
-            high.append((cos * d_re + sin * d_im, None))
-        else:
-            low.append((p_re + m_re, p_im + m_im))
-            high.append((cos * d_re + sin * d_im, cos * d_im - sin * d_re))
+        low.append((p_re + m_re, p_im + m_im))
+        high.append(turn(p_re - m_re, p_im - m_im, -theta / 2))
     return low + high
 
 
@@ -117,7 +117,7 @@
             tails[w, p] = across(pick, sources[w][at, tok - LANES :]).astype(BF16)
         return 0
 
-    lax.fori_loop(0, n, tail_step, 0)
+    lax.fori_loop(0, n, tail_step, 0, unroll=4)
 
     pl.semaphore_wait(barrier, n - 1)
     halo_copy = pltpu.make_async_remote_copy(
@@ -125,10 +125,6 @@
         device_id={"ctx": lax.rem(me + 1, n)}, device_id_type=MESH,
     )
 
-    for leaf in range(blocks):
-        for part in range(2):
-            column = twist_ref[:, part * blocks + leaf : part * blocks + leaf + 1]
-            twist[leaf, part] = jnp.broadcast_to(column, (LANES, lanes))
     halo_copy.start()
     if lanes < LANES:
         spec[...] = jnp.zeros_like(spec)
@@ -145,7 +141,7 @@
     def leaf_lanes(leaf):
         return slice((leaf % 2) * LANES, (leaf % 2) * LANES + lanes)
 
-    def short_stage(ref, c):
+    def short_stage(ref, c, first=False):
         at_lanes = chunk_lanes(c)
 
         def one(r, _):
@@ -153,6 +149,10 @@
             im_at = pl.ds(pl.multiple_of(LANES + r * step, step), step)
 
             def emit(leaf, re, im):
+                if first:
+                    for which in range(2):
+                        column = twist_ref[re_at, which * blocks + leaf : which * blocks + leaf + 1]
+                        twist[leaf, which, re_at, :] = jnp.broadcast_to(column, (step, lanes))
                 cos, sin = twist[leaf, 0, re_at, :], twist[leaf, 1, re_at, :]
                 spec[leaf // 2, re_at, leaf_lanes(leaf)] = (re * cos - im * sin).astype(BF16)
                 spec[leaf // 2, im_at, leaf_lanes(leaf)] = (re * sin + im * cos).astype(BF16)
@@ -160,14 +160,15 @@
             coefs = []
             for a in range(blocks):
                 at = pl.ds(pl.multiple_of((a % tiles) * LANES + r * step, step), step)
-                coefs.append((ref[a // tiles, at, at_lanes].astype(F32), None))
-            split_forward(coefs, math.pi / 2, 0, emit)
+                x, lean = ref[a // tiles, at, at_lanes].astype(F32), a * math.pi / (2 * blocks)
+                coefs.append((x * math.cos(lean), x * math.sin(lean)))
+            split_forward(coefs, 0.0, 0, emit)
             return 0
 
         lax.fori_loop(0, LANES // step, one, 0)
 
     def filter_chunk(c):
-        short_stage(filt_rows, c)
+        short_stage(filt_rows, c, c == 0)
 
         def filt_pair(pair, _):
             h_spec[c, pair] = jnp.dot(table_ref[0], spec[pair], preferred_element_type=F32).astype(h_spec.dtype)
@@ -181,12 +182,18 @@
     def peer_rows(peer, c):
         return pl.ds(pl.multiple_of(peer * chan + c * lanes, lanes), lanes)
 
-    def short(w, slot, peer, c):
-        turned[slot, :SLOT, :] = jnp.where(me > 0, halo[w, peer, :, chunk_lanes(c)].astype(F32), 0.0)
-        turned[slot, SLOT:, :] = across(eye[:tok, :tok], sources[w][peer_rows(peer, c), :])
-        if len(taps_ref.shape) == 3:
-            return taps_ref[w, :, peer_rows(peer, c)]
-        return taps_ref[peer, w, :, chunk_lanes(c)]
+    def short(first, pair, c):
+        block = jnp.concatenate([sources[w][peer_rows(peer, c), :] for w, peer in pair], axis=0)
+        both = across(eye[:tok, :tok], block)
+        taps = []
+        for i, (w, peer) in enumerate(pair):
+            turned[first + i, :SLOT, :] = jnp.where(me > 0, halo[w, peer, :, chunk_lanes(c)].astype(F32), 0.0)
+            turned[first + i, SLOT:, :] = both[:, i * lanes : (i + 1) * lanes]
+            if len(taps_ref.shape) == 3:
+                taps.append(taps_ref[w, :, peer_rows(peer, c)])
+            else:
+                taps.append(taps_ref[peer, w, :, chunk_lanes(c)])
+        return taps
 
     def sums_of(slot, taps, start, count):
         total = None
@@ -198,7 +205,7 @@
     part = 64
 
     def gate_pair(peers, c):
-        taps = [(short(1, 2 * i, p, c), short(2, 2 * i + 1, p, c)) for i, p in enumerate(peers)]
+        taps = [short(2 * i, [(1, p), (2, p)], c) for i, p in enumerate(peers)]
         for i, p in enumerate(peers):
             for start in range(0, tok, part):
                 product = sums_of(2 * i, taps[i][0], start, part) * sums_of(2 * i + 1, taps[i][1], start, part)
@@ -274,11 +281,13 @@
                 cos, sin = twist[leaf, 0, re_at, :], twist[leaf, 1, re_at, :]
                 return re * cos + im * sin, im * cos - re * sin
 
-            parts = split_inverse(fetch, blocks, math.pi / 2, 0, True)
-            for a, (re, _unused) in enumerate(parts):
+            parts = split_inverse(fetch, blocks, 0.0, 0)
+            for a, (re, im) in enumerate(parts):
+                lean = a * math.pi / (2 * blocks)
+                cos, sin = math.cos(lean) / length, math.sin(lean) / length
                 at = pl.ds(pl.multiple_of((a % tiles) * LANES + r * step, step), step)
                 sig = recv[a // tiles, at, at_lanes].astype(F32)
-                recv[a // tiles, at, at_lanes] = (re * (1.0 / length) + gain * sig).astype(BF16)
+                recv[a // tiles, at, at_lanes] = (cos * re + sin * im + gain * sig).astype(BF16)
             return 0
 
         lax.fori_loop(0, LANES // step, back_step, 0)
@@ -293,7 +302,7 @@
     for c in range(chunks):
         def q_step(i, _):
             peers = (2 * i, 2 * i + 1)
-            taps = [short(0, slot, p, c) for slot, p in enumerate(peers)]
+            taps = short(0, [(0, p) for p in peers], c)
             for slot, p in enumerate(peers):
                 parts = [sums_of(slot, taps[slot], start, part).astype(BF16) for start in range(0, tok, part)]
                 out_ref[peer_rows(p, c), :] = across(eye[:lanes, :lanes], jnp.concatenate(parts, axis=0)).astype(BF16)
@@ -328,7 +337,7 @@
         lanes = min(chan, LANES)
         chunks = chan // lanes
         table = jnp.asarray(circle_tables())
-        columns = jnp.asarray(twist_columns(blocks))
+        twist = jnp.asarray(twist_columns(blocks))
         dma = pltpu.SemaphoreType.DMA
         two = 2 * LANES
         small = blocks * two * max(chan, LANES) * 4 <= 8 * 2**20
@@ -368,7 +377,7 @@
                 collective_id=0, has_side_effects=True, vmem_limit_bytes=67043328
             ),
             name="hyena",
-        )(queries, keys, values, taps, long_filter[0], skip_gain, table, columns)
+        )(queries, keys, values, taps, long_filter[0], skip_gain, table, twist)
 
     placed = (
         P("ch", "ctx"),

time: 39.3 us -> 38.3 us (0.975)
  Pallas kernels: 36.8 us -> 35.8 us
    pallas_call x1, Pallas kernels: 36.8 us -> 35.8 us  [local(): pl.pallas_call(functools.partial(kernel, n, lanes), out_shape=jax.ShapeDt...]
where the time goes in v4:
time: 38.3 us; the launch traced here: 38.1 us
  Pallas kernels  35.8 us (93%)
  local copies, waits for them, and re-layouts  2.26 us (6%)
    pallas_call x1, Pallas kernels, local(): pl.pallas_call(functools.partial(kernel, n, lanes), out_shape=jax.ShapeDt...  35.8 us
    unnamed x1, local copies, waits for them, and re-layouts  2.26 us

profile of v4, /device:TPU:0, one launch (start us, length us, event | category | flops | bytes accessed | tf_op | source)
XLA Modules:
  0.0 38.1 jit_solution(16690472263436343095)
XLA Ops:
  0.0 35.8 %hyena.1 = bf16[2048,256]{1,0:T(8,128)(2,1)} custom-call(bf16[2048,256]{1,0:T(8,128)(2,1)} %q_ref.1, bf16[2048,256]{1,0:T(8,128)(2,1)} %k_ref.1, bf16[2048,256]{1,0:T(8,128)(2,1)} %v_ref.1, f32[3,7,2048]{2,1,0:T(8,128)} %taps_ref.1, bf16[256,2048]{1,0:T(8,128)(2,1)} %bitcast.1, f32[1,256]{1,0:T(1,128)} %gain_ref.1, ...), custom_call_target="tpu_custom_call" | custom-call | tf_op jit(solution)/shard_map/hyena/pallas_call | solution.py:349
  35.8 2.3 %copy.10 = bf16[2048,256]{1,0:T(8,128)(2,1)} copy(bf16[2048,256]{1,0:T(8,128)(2,1)} %hyena.1) | data formatting | bytes 2097152

commit v5 on v4

--- a/solution.py
+++ b/solution.py
@@ -83,9 +83,9 @@
 def kernel(
     n, lanes,
     q_ref, k_ref, v_ref, taps_ref, filt_hbm, gain_ref, table_ref, twist_ref,
-    out_ref,
-    eye, tails, halo, turned, gated, recv, spec, h_spec, ret, filt_ref, filt_rows, twist,
-    filt_sem, halo_sem, in_send, in_recv, in_own, out_send, out_recv, out_own,
+    out_hbm,
+    out_ref, eye, tails, halo, turned, gated, recv, spec, h_spec, ret, filt_ref, filt_rows, twist,
+    filt_sem, halo_sem, in_send, in_recv, in_own, out_send, out_recv, out_own, put,
 ):
     me = lax.axis_index("ctx")
     width, tok = q_ref.shape
@@ -314,6 +314,11 @@
         at = peer_rows(peer, c)
         long = across(eye[:lanes, :lanes], ret[peer, :, chunk_lanes(c)])
         out_ref[at, :] = (out_ref[at, :].astype(F32) * long).astype(BF16)
+        put_copy(peer, c).start()
+
+    def put_copy(peer, c):
+        at = peer_rows(peer, c)
+        return pltpu.make_async_copy(out_ref.at[at, :], out_hbm.at[at, :], put.at[c, peer])
 
     for c in range(chunks):
         own_out(c).wait()
@@ -325,6 +330,13 @@
             return 0
 
         lax.fori_loop(1, n, mix_step, 0)
+
+    for c in range(chunks):
+        def put_step(p, _):
+            put_copy(p, c).wait()
+            return 0
+
+        lax.fori_loop(0, n, put_step, 0)
 
 
 def solution(mesh):
@@ -350,8 +362,9 @@
             functools.partial(kernel, n, lanes),
             out_shape=jax.ShapeDtypeStruct((width, tok), BF16),
             in_specs=[any_space if i == 4 else pl.BlockSpec(memory_space=pltpu.VMEM) for i in range(8)],
-            out_specs=pl.BlockSpec(memory_space=pltpu.VMEM),
+            out_specs=any_space,
             scratch_shapes=[
+                pltpu.VMEM((width, tok), BF16),
                 pltpu.VMEM((side, side), BF16),
                 pltpu.VMEM((3, n, SLOT, chan), BF16),
                 pltpu.VMEM((3, n, SLOT, chan), BF16),
@@ -372,6 +385,7 @@
                 dma((chunks, n)),
                 dma((chunks, n)),
                 dma((chunks,)),
+                dma((chunks, n)),
             ],
             compiler_params=pltpu.CompilerParams(
                 collective_id=0, has_side_effects=True, vmem_limit_bytes=67043328

time: 38.3 us -> 38 us (level)
  no operation moved by 1% of the time
where the time goes in v5:
time: 38 us; the launch traced here: 37.8 us
  Pallas kernels  35.6 us (94%)
  local copies, waits for them, and re-layouts  2.26 us (6%)
    pallas_call x1, Pallas kernels, local(): pl.pallas_call(functools.partial(kernel, n, lanes), out_shape=jax.ShapeDt...  35.6 us
    unnamed x1, local copies, waits for them, and re-layouts  2.26 us

profile of v5, /device:TPU:0, one launch (start us, length us, event | category | flops | bytes accessed | tf_op | source)
XLA Modules:
  0.0 37.8 jit_solution(17076653858419255266)
XLA Ops:
  0.0 35.6 %hyena.1 = bf16[2048,256]{1,0:T(8,128)(2,1)} custom-call(bf16[2048,256]{1,0:T(8,128)(2,1)} %q_ref.1, bf16[2048,256]{1,0:T(8,128)(2,1)} %k_ref.1, bf16[2048,256]{1,0:T(8,128)(2,1)} %v_ref.1, f32[3,7,2048]{2,1,0:T(8,128)} %taps_ref.1, bf16[256,2048]{1,0:T(8,128)(2,1)} %bitcast.1, f32[1,256]{1,0:T(1,128)} %gain_ref.1, ...), custom_call_target="tpu_custom_call" | custom-call | tf_op jit(solution)/shard_map/hyena/pallas_call | solution.py:361
  35.6 2.3 %copy.10 = bf16[2048,256]{1,0:T(8,128)(2,1)} copy(bf16[2048,256]{1,0:T(8,128)(2,1)} %hyena.1) | data formatting | bytes 2097152
